TPU v7x, 32 devices: a whole 2x2x4 slice. The times are simulated.
32 devices in a mesh: ves: 4 (over x, core), shard: 8 (over z, y).
Axes of the slice: x: 2, y: 2, z: 4, core: 2. Of those that a mesh axis runs over, the one named last changes fastest.
Arguments:
- displacement: float32 [3, 8, 256, 128], P(None, 'ves', 'shard'), may hold values from -6 to 6
- tension: float32 [8], P('ves'), may hold values from 2 to 8
- bending: float32 [8], P('ves'), may hold values from 0.2 to 0.8
- offset: float32 [3, 8, 256, 128], P(None, 'ves', 'shard'), may hold values from 0 to 1
- owner: int32 [8, 256, 128], P('ves', 'shard'), may hold values from 0 to 31, as said below
- cell: int32 [8, 256, 128], P('ves', 'shard'), may hold values from 0 to 131071
- populations: float32 [64, 19, 256, 256], P(('ves', 'shard')), may hold values from 0 to 1, as said below
Outputs:
- membrane_force: float32 [3, 8, 256, 128], P(None, 'ves', 'shard')
- force_field: float32 [64, 3, 256, 256], P(('ves', 'shard'))
- new_populations: float32 [64, 19, 256, 256], P(('ves', 'shard'))
Inputs may be any that keep to these rules, and one draw needn't show every extreme that they name: The points of one device name any one owner at most 512 times, and some owner is named exactly 512 times by the points of every device. `populations`: entries are positive.
All inputs are finite; a program needn't handle non-finite values.
Results may differ from a plain program's by a relative error of at most 0.0061.
Values sent between devices are 32-bit elements; how exact they have to be, the bound alone decides.
A program may use at most 128 MiB of HBM per device.

v0:
```python
import math

import jax
import jax.numpy as jnp
from jax import lax
from jax.sharding import PartitionSpec as P

relax_time = 0.8
velocity_x = [0, 1, -1, 0, 0, 0, 1, -1, 0, 0, 0, 1, -1, 0, 0, 1, 1, -1, -1]
velocity_y = [0, 0, 0, 1, -1, 0, 0, 0, 1, -1, 0, 0, 0, 1, -1, 1, -1, 1, -1]
velocity_z = [1, 1, 1, 1, 1, -1, -1, -1, -1, -1, 0, 0, 0, 0, 0, 0, 0, 0, 0]
lattice_weights = [
    1.0 / 18,
    1.0 / 36,
    1.0 / 36,
    1.0 / 36,
    1.0 / 36,
    1.0 / 18,
    1.0 / 36,
    1.0 / 36,
    1.0 / 36,
    1.0 / 36,
    1.0 / 3,
    1.0 / 18,
    1.0 / 18,
    1.0 / 18,
    1.0 / 18,
    1.0 / 36,
    1.0 / 36,
    1.0 / 36,
    1.0 / 36,
]


def padded_2(x, sides, width):
    for axis, dim in sides:
        devices, length = (lax.axis_size(axis), x.shape[dim])
        up = [(i, (i + 1) % devices) for i in range(devices - 1)]
        down = [(j, i) for i, j in up]
        last = lax.slice_in_dim(x, length - width, length, axis=dim)
        initial = lax.slice_in_dim(x, 0, width, axis=dim)
        before = lax.ppermute(last, axis, up)
        after = lax.ppermute(initial, axis, down)
        x = jnp.concatenate([before, x, after], axis=dim)
    return x


def passed_along(value, axis, steps):
    count = lax.axis_size(axis)
    pairs = [(source, (source + steps) % count) for source in range(count)]
    return lax.ppermute(value, axis, pairs)


def kernel_weight(distance):
    return 0.25 * (1.0 + jnp.cos(0.5 * math.pi * distance))


def surface_laplacian(padded):
    center = padded[:, :, 1:-1]
    return (
        padded[:, :, 2:]
        + padded[:, :, :-2]
        + jnp.roll(center, 1, 3)
        + jnp.roll(center, -1, 3)
        - 4.0 * center
    )


def collide(populations, field):
    density = jnp.sum(populations, 1)
    moment_x = jnp.zeros_like(density)
    moment_y = jnp.zeros_like(density)
    moment_z = jnp.zeros_like(density)
    for item in range(19):
        moment_x = moment_x + velocity_x[item] * populations[:, item]
        moment_y = moment_y + velocity_y[item] * populations[:, item]
        moment_z = moment_z + velocity_z[item] * populations[:, item]
    flow_x = (moment_x + 0.5 * field[:, 0]) / density
    flow_y = (moment_y + 0.5 * field[:, 1]) / density
    flow_z = (moment_z + 0.5 * field[:, 2]) / density
    speed_sq = flow_x * flow_x + flow_y * flow_y + flow_z * flow_z
    result = []
    for item in range(19):
        ex, ey, ez = (velocity_x[item], velocity_y[item], velocity_z[item])
        weight = lattice_weights[item]
        along = ex * flow_x + ey * flow_y + ez * flow_z
        equilibrium = weight * density * (1.0 + 3.0 * along + 4.5 * along * along - 1.5 * speed_sq)
        push = (
            (ex - flow_x) * field[:, 0] + (ey - flow_y) * field[:, 1] + (ez - flow_z) * field[:, 2]
        )
        facing = ex * field[:, 0] + ey * field[:, 1] + ez * field[:, 2]
        source = weight * (3.0 * push + 9.0 * along * facing)
        current = populations[:, item]
        result.append(
            current - (current - equilibrium) / relax_time + (1.0 - 0.5 / relax_time) * source
        )
    return jnp.stack(result, 1)


def on_device(displacement, tension, bending, offset, owner, cell, populations):
    padded = padded_2(displacement, (("shard", 2),), 1)
    first = surface_laplacian(padded)
    padded_first = padded_2(first, (("shard", 2),), 1)
    second = surface_laplacian(padded_first)
    membrane_force = tension[None, :, None, None] * first - bending[None, :, None, None] * second
    ves_count = lax.axis_size("ves")
    shard_count = lax.axis_size("shard")
    device_count = ves_count * shard_count
    point_count = owner.size
    capacity = 2 * point_count // device_count
    slot_total = device_count * capacity
    payload = jnp.concatenate(
        [membrane_force.reshape(3, point_count), offset.reshape(3, point_count)], 0
    )
    owner_flat = owner.reshape(point_count)
    cell_flat = cell.reshape(point_count)
    order = jnp.argsort(owner_flat, stable=True)
    sorted_owner = owner_flat[order]
    matches = sorted_owner[:, None] == jnp.arange(device_count, dtype=jnp.int32)[None, :]
    counts = jnp.sum(matches.astype(jnp.int32), 0)
    starts = jnp.cumsum(counts) - counts
    first_place = jnp.sum(jnp.where(matches, starts[None, :], 0), 1)
    slot = sorted_owner * capacity + jnp.arange(point_count, dtype=jnp.int32) - first_place
    send_values = jnp.zeros((6, slot_total), jnp.float32).at[:, slot].set(payload[:, order])
    send_cells = jnp.zeros((1, slot_total), jnp.int32).at[0, slot].set(cell_flat[order])
    got_values, got_cells = (
        lax.all_to_all(
            send_values.reshape(6, device_count, capacity),
            ("ves", "shard"),
            split_axis=1,
            concat_axis=1,
            tiled=True,
        ),
        lax.all_to_all(
            send_cells.reshape(1, device_count, capacity),
            ("ves", "shard"),
            split_axis=1,
            concat_axis=1,
            tiled=True,
        ),
    )
    got_values = got_values.reshape(6, slot_total)
    got_cells = got_cells.reshape(slot_total)
    slab = populations.shape[0]
    width = populations.shape[2]
    depth = slab + 3
    block = min(1024, slot_total)
    turns = slot_total // block
    value_blocks = got_values.reshape(6, turns, block).transpose(1, 0, 2)
    cell_blocks = got_cells.reshape(turns, block)
    grid = jnp.arange(width, dtype=jnp.int32)
    layers = jnp.arange(depth, dtype=jnp.int32)

    def spread_block(total, items):
        values, cells = items
        plane = cells // (width * width)
        column_x = cells // width % width
        column_y = cells % width
        weight_x = jnp.zeros((block, width), jnp.float32)
        weight_y = jnp.zeros((block, width), jnp.float32)
        weight_z = jnp.zeros((block, depth), jnp.float32)
        for reach in range(-1, 3):
            weight_x = weight_x + jnp.where(
                grid[None, :] == ((column_x + reach) % width)[:, None],
                kernel_weight(values[3] - reach)[:, None],
                0.0,
            )
            weight_y = weight_y + jnp.where(
                grid[None, :] == ((column_y + reach) % width)[:, None],
                kernel_weight(values[4] - reach)[:, None],
                0.0,
            )
            weight_z = weight_z + jnp.where(
                layers[None, :] == (plane + reach + 1)[:, None],
                kernel_weight(values[5] - reach)[:, None],
                0.0,
            )
        scaled = values[0:3].T[:, None, :, None] * weight_z[:, :, None, None]
        left = (
            (scaled * weight_x[:, None, None, :])
            .astype(jnp.bfloat16)
            .reshape(block, depth * 3 * width)
        )
        right = weight_y.astype(jnp.bfloat16)
        product = lax.dot_general(
            left, right, (((0,), (0,)), ((), ())), preferred_element_type=jnp.float32
        )
        return (total + product, None)

    total, unused = lax.scan(
        spread_block,
        jnp.zeros((depth * 3 * width, width), jnp.float32),
        (value_blocks, cell_blocks),
    )
    spread = total.reshape(depth, 3, width, width)
    from_below = passed_along(spread[slab + 1 : slab + 3], ("ves", "shard"), 1)
    from_above = passed_along(spread[0:1], ("ves", "shard"), -1)
    force_field = spread[1 : slab + 1].at[0:2].add(from_below).at[slab - 1 : slab].add(from_above)
    post = collide(populations, force_field)
    low_part = passed_along(post[slab - 1, 0:5], ("ves", "shard"), 1)
    high_part = passed_along(post[0, 5:10], ("ves", "shard"), -1)
    low_source = jnp.concatenate([low_part[None], post[: slab - 1, 0:5]], 0)
    high_source = jnp.concatenate([post[1:, 5:10], high_part[None]], 0)
    source = jnp.concatenate([low_source, high_source, post[:, 10:]], 1)
    moved = [
        jnp.roll(source[:, item], (velocity_x[item], velocity_y[item]), (1, 2))
        for item in range(19)
    ]
    return (membrane_force, force_field, jnp.stack(moved, 1))


def solution(mesh):
    return jax.shard_map(
        on_device,
        mesh=mesh,
        in_specs=(
            P(None, "ves", "shard", None),
            P("ves"),
            P("ves"),
            P(None, "ves", "shard", None),
            P("ves", "shard", None),
            P("ves", "shard", None),
            P(("ves", "shard"), None, None, None),
        ),
        out_specs=(
            P(None, "ves", "shard", None),
            P(("ves", "shard"), None, None, None),
            P(("ves", "shard"), None, None, None),
        ),
        check_vma=False,
    )
```

profile of v0, /device:TPU:14, one launch (start us, length us, event | category | flops | bytes accessed | tf_op | source)
XLA Modules:
  0.0 647.5 jit_solution(11068581569204606611)
XLA Ops:
  14.9 45.5 %gather_fusion = s32[8192]{0:T(1024)S(1)} fusion(s32[8192]{0:T(1024)S(1)} %bitcast.1381, s32[8192]{0:T(1024)S(1)} %fusion.372), kind=kCustom, calls=%fused_computation | custom fusion | bytes 98304 | tf_op jit(solution)/shard_map/gather | solution.py:118
  61.6 45.5 %gather_fusion.1 = s32[8192]{0:T(1024)S(1)} fusion(s32[8192]{0:T(1024)S(1)} %bitcast.1379, s32[8192]{0:T(1024)S(1)} %fusion.372), kind=kCustom, calls=%fused_computation.2 | custom fusion | bytes 98304 | tf_op jit(solution)/shard_map/gather | solution.py:125
  107.2 31.1 %scatter_custom_fusion.1 = s32[16384]{0:T(1024)} fusion(s32[8192]{0:T(1024)S(1)} %broadcast_select_fusion, s32[8192]{0:T(1024)S(1)} %gather_fusion.1, s32[]{:T(128)} %constant.337.clone.1), kind=kCustom, calls=%fused_computation.665 | custom fusion | bytes 65540
  157.5 70.4 %scatter_custom_fusion = f32[6,16384]{0,1:T(8,128)} fusion(s32[8192]{0:T(1024)S(1)} %bitcast.1413, f32[6,8192]{0,1:T(8,128)} %copy.148, s32[8192]{0:T(1024)S(1)} %fusion.372, f32[]{:T(128)} %constant.338.clone.1), kind=kCustom, calls=%fused_computation.104 | custom fusion | bytes 393728 | tf_op jit(solution)/shard_map/scatter | solution.py:124
  239.3 13.1 %all-to-all-done = f32[6,32,512]{2,0,1:T(8,128)S(1)} async-done(((f32[6,32,512]{2,0,1:T(8,128)}), f32[6,32,512]{2,0,1:T(8,128)S(1)}, u32[]{:S(2)}, u32[]{:S(2)}) %all-to-all-start) | async-done | bytes 393248 | tf_op jit(solution)/shard_map/all_to_all | solution.py:127
  252.7 253.5 %while.18 = (s32[]{:T(128)}, f32[3840,256]{1,0:T(8,128)}, f32[16,6,1024]{2,0,1:T(8,128)S(1)}, s32[16,1024]{1,0:T(8,128)S(1)}, s32[]{:T(128)}, /*index=5*/s32[]{:T(128)}, s32[]{}, s32[]{}, s32[]{}) while((s32[]{:T(128)}, f32[3840,256]{1,0:T(8,128)}, f32[16,6,1024]{2,0,1:T(8,128)S(1)}, s32[16,1024]{1,0:T(8,128)S(1)}, ...), condition=%wide.region_7.8_spmd.clone.clone, body=%wide.region_6.7_spmd.clone.clone.sunk | while | flops 2029383680 | bytes 26144940 | solution.py:190
  260.0 7.5 %convolution_add_fusion.2 = f32[3840,256]{1,0:T(8,128)} fusion(bf16[1024,3840]{0,1:T(8,128)(2,1)} %bitcast.1382, f32[3840,256]{1,0:T(8,128)} %get-tuple-element.434, pred[]{:T(512)S(6)} %compare.117, f32[1024]{0:T(1024)S(1)} %bitcast.1419, s32[1024]{0:T(1024)S(1)} %get-tuple-element.417, f32[1024]{0:T(1024)S(1)} %bitcast.1418, ...), kind=kOutput, calls=%fused_computation.8.clone.1 | convolution fusion | flops 2018377728 | bytes 15761409 | tf_op jit(solution)/shard_map/while/body/eval_jaxpr/dot_general | solution.py:185
  274.8 8.6 %convolution_add_fusion.2 = f32[3840,256]{1,0:T(8,128)} fusion(bf16[1024,3840]{0,1:T(8,128)(2,1)} %bitcast.1382, f32[3840,256]{1,0:T(8,128)} %get-tuple-element.434, pred[]{:T(512)S(6)} %compare.117, f32[1024]{0:T(1024)S(1)} %bitcast.1419, s32[1024]{0:T(1024)S(1)} %get-tuple-element.417, f32[1024]{0:T(1024)S(1)} %bitcast.1418, ...), kind=kOutput, calls=%fused_computation.8.clone.1 | convolution fusion | flops 2018377728 | bytes 15761409 | tf_op jit(solution)/shard_map/while/body/eval_jaxpr/dot_general | solution.py:185
  290.7 8.6 %convolution_add_fusion.2 = f32[3840,256]{1,0:T(8,128)} fusion(bf16[1024,3840]{0,1:T(8,128)(2,1)} %bitcast.1382, f32[3840,256]{1,0:T(8,128)} %get-tuple-element.434, pred[]{:T(512)S(6)} %compare.117, f32[1024]{0:T(1024)S(1)} %bitcast.1419, s32[1024]{0:T(1024)S(1)} %get-tuple-element.417, f32[1024]{0:T(1024)S(1)} %bitcast.1418, ...), kind=kOutput, calls=%fused_computation.8.clone.1 | convolution fusion | flops 2018377728 | bytes 15761409 | tf_op jit(solution)/shard_map/while/body/eval_jaxpr/dot_general | solution.py:185
  306.6 8.6 %convolution_add_fusion.2 = f32[3840,256]{1,0:T(8,128)} fusion(bf16[1024,3840]{0,1:T(8,128)(2,1)} %bitcast.1382, f32[3840,256]{1,0:T(8,128)} %get-tuple-element.434, pred[]{:T(512)S(6)} %compare.117, f32[1024]{0:T(1024)S(1)} %bitcast.1419, s32[1024]{0:T(1024)S(1)} %get-tuple-element.417, f32[1024]{0:T(1024)S(1)} %bitcast.1418, ...), kind=kOutput, calls=%fused_computation.8.clone.1 | convolution fusion | flops 2018377728 | bytes 15761409 | tf_op jit(solution)/shard_map/while/body/eval_jaxpr/dot_general | solution.py:185
  322.5 8.6 %convolution_add_fusion.2 = f32[3840,256]{1,0:T(8,128)} fusion(bf16[1024,3840]{0,1:T(8,128)(2,1)} %bitcast.1382, f32[3840,256]{1,0:T(8,128)} %get-tuple-element.434, pred[]{:T(512)S(6)} %compare.117, f32[1024]{0:T(1024)S(1)} %bitcast.1419, s32[1024]{0:T(1024)S(1)} %get-tuple-element.417, f32[1024]{0:T(1024)S(1)} %bitcast.1418, ...), kind=kOutput, calls=%fused_computation.8.clone.1 | convolution fusion | flops 2018377728 | bytes 15761409 | tf_op jit(solution)/shard_map/while/body/eval_jaxpr/dot_general | solution.py:185
  338.4 8.6 %convolution_add_fusion.2 = f32[3840,256]{1,0:T(8,128)} fusion(bf16[1024,3840]{0,1:T(8,128)(2,1)} %bitcast.1382, f32[3840,256]{1,0:T(8,128)} %get-tuple-element.434, pred[]{:T(512)S(6)} %compare.117, f32[1024]{0:T(1024)S(1)} %bitcast.1419, s32[1024]{0:T(1024)S(1)} %get-tuple-element.417, f32[1024]{0:T(1024)S(1)} %bitcast.1418, ...), kind=kOutput, calls=%fused_computation.8.clone.1 | convolution fusion | flops 2018377728 | bytes 15761409 | tf_op jit(solution)/shard_map/while/body/eval_jaxpr/dot_general | solution.py:185
  354.4 8.6 %convolution_add_fusion.2 = f32[3840,256]{1,0:T(8,128)} fusion(bf16[1024,3840]{0,1:T(8,128)(2,1)} %bitcast.1382, f32[3840,256]{1,0:T(8,128)} %get-tuple-element.434, pred[]{:T(512)S(6)} %compare.117, f32[1024]{0:T(1024)S(1)} %bitcast.1419, s32[1024]{0:T(1024)S(1)} %get-tuple-element.417, f32[1024]{0:T(1024)S(1)} %bitcast.1418, ...), kind=kOutput, calls=%fused_computation.8.clone.1 | convolution fusion | flops 2018377728 | bytes 15761409 | tf_op jit(solution)/shard_map/while/body/eval_jaxpr/dot_general | solution.py:185
  370.3 8.6 %convolution_add_fusion.2 = f32[3840,256]{1,0:T(8,128)} fusion(bf16[1024,3840]{0,1:T(8,128)(2,1)} %bitcast.1382, f32[3840,256]{1,0:T(8,128)} %get-tuple-element.434, pred[]{:T(512)S(6)} %compare.117, f32[1024]{0:T(1024)S(1)} %bitcast.1419, s32[1024]{0:T(1024)S(1)} %get-tuple-element.417, f32[1024]{0:T(1024)S(1)} %bitcast.1418, ...), kind=kOutput, calls=%fused_computation.8.clone.1 | convolution fusion | flops 2018377728 | bytes 15761409 | tf_op jit(solution)/shard_map/while/body/eval_jaxpr/dot_general | solution.py:185
  386.2 8.6 %convolution_add_fusion.2 = f32[3840,256]{1,0:T(8,128)} fusion(bf16[1024,3840]{0,1:T(8,128)(2,1)} %bitcast.1382, f32[3840,256]{1,0:T(8,128)} %get-tuple-element.434, pred[]{:T(512)S(6)} %compare.117, f32[1024]{0:T(1024)S(1)} %bitcast.1419, s32[1024]{0:T(1024)S(1)} %get-tuple-element.417, f32[1024]{0:T(1024)S(1)} %bitcast.1418, ...), kind=kOutput, calls=%fused_computation.8.clone.1 | convolution fusion | flops 2018377728 | bytes 15761409 | tf_op jit(solution)/shard_map/while/body/eval_jaxpr/dot_general | solution.py:185
  402.1 8.6 %convolution_add_fusion.2 = f32[3840,256]{1,0:T(8,128)} fusion(bf16[1024,3840]{0,1:T(8,128)(2,1)} %bitcast.1382, f32[3840,256]{1,0:T(8,128)} %get-tuple-element.434, pred[]{:T(512)S(6)} %compare.117, f32[1024]{0:T(1024)S(1)} %bitcast.1419, s32[1024]{0:T(1024)S(1)} %get-tuple-element.417, f32[1024]{0:T(1024)S(1)} %bitcast.1418, ...), kind=kOutput, calls=%fused_computation.8.clone.1 | convolution fusion | flops 2018377728 | bytes 15761409 | tf_op jit(solution)/shard_map/while/body/eval_jaxpr/dot_general | solution.py:185
  418.0 8.6 %convolution_add_fusion.2 = f32[3840,256]{1,0:T(8,128)} fusion(bf16[1024,3840]{0,1:T(8,128)(2,1)} %bitcast.1382, f32[3840,256]{1,0:T(8,128)} %get-tuple-element.434, pred[]{:T(512)S(6)} %compare.117, f32[1024]{0:T(1024)S(1)} %bitcast.1419, s32[1024]{0:T(1024)S(1)} %get-tuple-element.417, f32[1024]{0:T(1024)S(1)} %bitcast.1418, ...), kind=kOutput, calls=%fused_computation.8.clone.1 | convolution fusion | flops 2018377728 | bytes 15761409 | tf_op jit(solution)/shard_map/while/body/eval_jaxpr/dot_general | solution.py:185
  433.9 8.6 %convolution_add_fusion.2 = f32[3840,256]{1,0:T(8,128)} fusion(bf16[1024,3840]{0,1:T(8,128)(2,1)} %bitcast.1382, f32[3840,256]{1,0:T(8,128)} %get-tuple-element.434, pred[]{:T(512)S(6)} %compare.117, f32[1024]{0:T(1024)S(1)} %bitcast.1419, s32[1024]{0:T(1024)S(1)} %get-tuple-element.417, f32[1024]{0:T(1024)S(1)} %bitcast.1418, ...), kind=kOutput, calls=%fused_computation.8.clone.1 | convolution fusion | flops 2018377728 | bytes 15761409 | tf_op jit(solution)/shard_map/while/body/eval_jaxpr/dot_general | solution.py:185
  449.8 8.6 %convolution_add_fusion.2 = f32[3840,256]{1,0:T(8,128)} fusion(bf16[1024,3840]{0,1:T(8,128)(2,1)} %bitcast.1382, f32[3840,256]{1,0:T(8,128)} %get-tuple-element.434, pred[]{:T(512)S(6)} %compare.117, f32[1024]{0:T(1024)S(1)} %bitcast.1419, s32[1024]{0:T(1024)S(1)} %get-tuple-element.417, f32[1024]{0:T(1024)S(1)} %bitcast.1418, ...), kind=kOutput, calls=%fused_computation.8.clone.1 | convolution fusion | flops 2018377728 | bytes 15761409 | tf_op jit(solution)/shard_map/while/body/eval_jaxpr/dot_general | solution.py:185
  465.8 8.6 %convolution_add_fusion.2 = f32[3840,256]{1,0:T(8,128)} fusion(bf16[1024,3840]{0,1:T(8,128)(2,1)} %bitcast.1382, f32[3840,256]{1,0:T(8,128)} %get-tuple-element.434, pred[]{:T(512)S(6)} %compare.117, f32[1024]{0:T(1024)S(1)} %bitcast.1419, s32[1024]{0:T(1024)S(1)} %get-tuple-element.417, f32[1024]{0:T(1024)S(1)} %bitcast.1418, ...), kind=kOutput, calls=%fused_computation.8.clone.1 | convolution fusion | flops 2018377728 | bytes 15761409 | tf_op jit(solution)/shard_map/while/body/eval_jaxpr/dot_general | solution.py:185
  481.7 8.6 %convolution_add_fusion.2 = f32[3840,256]{1,0:T(8,128)} fusion(bf16[1024,3840]{0,1:T(8,128)(2,1)} %bitcast.1382, f32[3840,256]{1,0:T(8,128)} %get-tuple-element.434, pred[]{:T(512)S(6)} %compare.117, f32[1024]{0:T(1024)S(1)} %bitcast.1419, s32[1024]{0:T(1024)S(1)} %get-tuple-element.417, f32[1024]{0:T(1024)S(1)} %bitcast.1418, ...), kind=kOutput, calls=%fused_computation.8.clone.1 | convolution fusion | flops 2018377728 | bytes 15761409 | tf_op jit(solution)/shard_map/while/body/eval_jaxpr/dot_general | solution.py:185
  497.6 8.6 %convolution_add_fusion.2 = f32[3840,256]{1,0:T(8,128)} fusion(bf16[1024,3840]{0,1:T(8,128)(2,1)} %bitcast.1382, f32[3840,256]{1,0:T(8,128)} %get-tuple-element.434, pred[]{:T(512)S(6)} %compare.117, f32[1024]{0:T(1024)S(1)} %bitcast.1419, s32[1024]{0:T(1024)S(1)} %get-tuple-element.417, f32[1024]{0:T(1024)S(1)} %bitcast.1418, ...), kind=kOutput, calls=%fused_computation.8.clone.1 | convolution fusion | flops 2018377728 | bytes 15761409 | tf_op jit(solution)/shard_map/while/body/eval_jaxpr/dot_general | solution.py:185
  518.1 45.2 %collective-permute-done.4 = f32[2,3,256,256]{3,2,1,0:T(8,128)} collective-permute-done((f32[2,3,256,256]{3,2,1,0:T(8,128)}, f32[2,3,256,256]{3,2,1,0:T(8,128)}, u32[]{:S(2)}, u32[]{:S(2)}) %collective-permute-start.4) | collective-permute-done | bytes 1572896 | tf_op jit(solution)/shard_map/ppermute | solution.py:51
  589.0 50.0 %collective-permute-done.6 = f32[5,256,256]{2,1,0:T(8,128)S(1)} collective-permute-done((f32[5,256,256]{2,1,0:T(8,128)S(1)}, f32[5,256,256]{2,1,0:T(8,128)S(1)}, u32[]{:S(2)}, u32[]{:S(2)}) %collective-permute-start.6) | collective-permute-done | bytes 1310752 | tf_op jit(solution)/shard_map/ppermute | solution.py:51
  (304 shorter events, 206.5 us)
Async XLA Ops:
  0.6 61.0 %copy-start = (s32[2,32,128]{2,1,0:T(8,128)S(1)}, s32[2,32,128]{2,1,0:T(8,128)}, u32[]{:S(2)}) copy-start(s32[2,32,128]{2,1,0:T(8,128)} %param.20) | copy-start | bytes 98308
  0.6 14.2 %copy-start.2 = (s32[2,32,128]{2,1,0:T(8,128)S(1)}, s32[2,32,128]{2,1,0:T(8,128)}, u32[]{:S(2)}) copy-start(s32[2,32,128]{2,1,0:T(8,128)} %param.19) | copy-start | bytes 98308
  1.4 143.0 %collective-permute-start.1 = (f32[3,2,1,128]{3,2,1,0:T(1,128)S(1)}, f32[3,2,1,128]{3,2,1,0:T(1,128)S(1)}, u32[]{:S(2)}, u32[]{:S(2)}) collective-permute-start(f32[3,2,1,128]{3,2,1,0:T(1,128)S(1)} %get-tuple-element.346), channel_id=1, source_target_pairs={{0,1},{1,2},{2,3},{3,4},{4,5},{5,6},{6,7},{8,9},{9,10},{10,11},{11... | collective-permute-start | bytes 9224 | tf_op jit(solution)/shard_map/ppermute | solution.py:42
  4.9 139.6 %collective-permute-start = (f32[3,2,1,128]{3,2,1,0:T(1,128)S(1)}, f32[3,2,1,128]{3,2,1,0:T(1,128)S(1)}, u32[]{:S(2)}, u32[]{:S(2)}) collective-permute-start(f32[3,2,1,128]{3,2,1,0:T(1,128)S(1)} %get-tuple-element.345), channel_id=1, source_target_pairs={{1,0},{2,1},{3,2},{4,3},{5,4},{6,5},{7,6},{9,8},{10,9},{11,10},{12... | collective-permute-start | bytes 9224 | tf_op jit(solution)/shard_map/ppermute | solution.py:43
  14.8 46.4 %copy-start.11 = (s32[2]{0:T(128)S(1)}, s32[2]{0:T(128)}, u32[]{:S(2)}) copy-start(s32[2]{0:T(128)} %constant.369) | copy-start | bytes 28
  14.8 46.6 %copy-start.10 = (s32[2]{0:T(128)S(1)}, s32[2]{0:T(128)}, u32[]{:S(2)}) copy-start(s32[2]{0:T(128)} %constant.366) | copy-start | bytes 28
  61.6 82.6 %copy-start.4 = (f32[3,2,32,128]{3,2,1,0:T(8,128)S(1)}, f32[3,2,32,128]{3,2,1,0:T(8,128)}, u32[]{:S(2)}) copy-start(f32[3,2,32,128]{3,2,1,0:T(8,128)} %param.15) | copy-start | bytes 294916
  61.6 92.8 %copy-start.8 = (f32[2]{0:T(128)S(1)}, f32[2]{0:T(128)}, u32[]{:S(2)}) copy-start(f32[2]{0:T(128)} %param.17) | copy-start | bytes 28
  61.6 92.8 %copy-start.9 = (f32[2]{0:T(128)S(1)}, f32[2]{0:T(128)}, u32[]{:S(2)}) copy-start(f32[2]{0:T(128)} %param.16) | copy-start | bytes 28
  61.6 93.0 %copy-start.6 = (f32[3,2,32,128]{3,2,1,0:T(8,128)S(1)}, f32[3,2,32,128]{3,2,1,0:T(8,128)}, u32[]{:S(2)}) copy-start(f32[3,2,32,128]{3,2,1,0:T(8,128)} %param.18) | copy-start | bytes 294916
  138.3 95.6 %all-to-all-start.1 = ((s32[1,32,512]{2,0,1:T(1,128)}), s32[1,32,512]{2,0,1:T(1,128)S(1)}, u32[]{:S(2)}, u32[]{:S(2)}) async-start(s32[1,32,512]{2,0,1:T(1,128)} %bitcast.8), calls=%async_computation.1 | async-start | bytes 131072 | tf_op jit(solution)/shard_map/all_to_all | solution.py:134
  144.7 6.0 collective-permute-start.3
  148.0 6.4 collective-permute-start.2
  154.6 73.3 %copy-start.5 = (f32[3,2,32,128]{3,2,1,0:T(8,128)}, f32[3,2,32,128]{3,2,1,0:T(8,128)S(1)}, u32[]{:S(2)}) copy-start(f32[3,2,32,128]{3,2,1,0:T(8,128)S(1)} %fusion.366) | copy-start | bytes 294916
  233.9 18.5 %all-to-all-start = ((f32[6,32,512]{2,0,1:T(8,128)}), f32[6,32,512]{2,0,1:T(8,128)S(1)}, u32[]{:S(2)}, u32[]{:S(2)}) async-start(f32[6,32,512]{2,0,1:T(8,128)} %copy.149), calls=%async_computation | async-start | bytes 1048576 | tf_op jit(solution)/shard_map/all_to_all | solution.py:127
  510.0 53.3 %collective-permute-start.4 = (f32[2,3,256,256]{3,2,1,0:T(8,128)}, f32[2,3,256,256]{3,2,1,0:T(8,128)}, u32[]{:S(2)}, u32[]{:S(2)}) collective-permute-start(f32[2,3,256,256]{3,2,1,0:T(8,128)} %bitcast.10), channel_id=1, source_target_pairs={{0,1},{1,2},{2,3},{3,4},{4,5},{5,6},{6,7},{7,8},{8,9},{9,10},{10,1... | collective-permute-start | bytes 4718600 | tf_op jit(solution)/shard_map/ppermute | solution.py:51
  511.2 54.4 %collective-permute-start.5 = (f32[1,3,256,256]{3,2,1,0:T(8,128)S(1)}, f32[1,3,256,256]{3,2,1,0:T(8,128)}, u32[]{:S(2)}, u32[]{:S(2)}) collective-permute-start(f32[1,3,256,256]{3,2,1,0:T(8,128)S(1)} %bitcast.1401), channel_id=1, source_target_pairs={{0,31},{1,0},{2,1},{3,2},{4,3},{5,4},{6,5},{7,6},{8,7},{9,8},{10,9... | collective-permute-start | bytes 2359304 | tf_op jit(solution)/shard_map/ppermute | solution.py:51
  513.5 59.4 %slice-start = ((s8[9961472]{0:T(1024)(128)(4,1)}), s8[1572864]{0:T(1024)(128)(4,1)S(1)}, s32[]{:S(2)}) async-start(s8[9961472]{0:T(1024)(128)(4,1)} %bitcast.1383), calls=%async_computation.2 | async-start | bytes 3145728
  563.3 9.6 %slice-start.1 = ((s8[9961472]{0:T(1024)(128)(4,1)}), s8[4194304]{0:T(1024)(128)(4,1)S(1)}, s32[]{:S(2)}) async-start(s8[9961472]{0:T(1024)(128)(4,1)} %bitcast.1383), calls=%async_computation.3 | async-start | bytes 8388608
  566.9 74.4 %copy-start.3 = (f32[2,3,256,256]{3,2,1,0:T(8,128)}, f32[2,3,256,256]{3,2,1,0:T(8,128)S(1)}, u32[]{:S(2)}) copy-start(f32[2,3,256,256]{3,2,1,0:T(8,128)S(1)} %fusion.29) | copy-start | bytes 4718596
  566.9 6.0 slice-start.2
  580.3 59.8 %collective-permute-start.7 = (f32[5,256,256]{2,1,0:T(8,128)S(1)}, f32[5,256,256]{2,1,0:T(8,128)S(1)}, u32[]{:S(2)}, u32[]{:S(2)}) collective-permute-start(f32[5,256,256]{2,1,0:T(8,128)S(1)} %get-tuple-element.327), channel_id=1, source_target_pairs={{0,31},{1,0},{2,1},{3,2},{4,3},{5,4},{6,5},{7,6},{8,7},{9,8},{10,9... | collective-permute-start | bytes 3932168 | tf_op jit(solution)/shard_map/ppermute | solution.py:51
  580.9 58.1 %collective-permute-start.6 = (f32[5,256,256]{2,1,0:T(8,128)S(1)}, f32[5,256,256]{2,1,0:T(8,128)S(1)}, u32[]{:S(2)}, u32[]{:S(2)}) collective-permute-start(f32[5,256,256]{2,1,0:T(8,128)S(1)} %get-tuple-element.334), channel_id=1, source_target_pairs={{0,1},{1,2},{2,3},{3,4},{4,5},{5,6},{6,7},{7,8},{8,9},{9,10},{10,1... | collective-permute-start | bytes 3932168 | tf_op jit(solution)/shard_map/ppermute | solution.py:51
  642.0 5.0 copy-start.1
  (1 other events, 3.9 us)
where the time goes:
time: 660 us; the launch traced here: 647 us
  local copies, waits for them, and re-layouts  214 us (32%)
  other arithmetic  153 us (23%)
  matrix products  137 us (21%)
  waiting for transfers between devices  112 us (17%)
  starting transfers between devices  28.4 us (4%)
    dot_general x16, matrix products, spread_block(): lax.dot_general(left, right, (((0,), (0,)), ((), ())), preferred_element_...  137 us
    ppermute x4, waiting for transfers between devices, passed_along(): return lax.ppermute(value, axis, pairs)  95.2 us
    convert_element_type x16, other arithmetic, spread_block(): left = (scaled * weight_x[:, None, None, :]).astype(jnp.bfloat16).reshape...  86.4 us
    scatter x1, local copies, waits for them, and re-layouts, on_device(): jnp.zeros((6, slot_total), jnp.float32).at[:, slot].set(payload[:, order])  70.4 us
    gather x1, local copies, waits for them, and re-layouts, on_device(): sorted_owner = owner_flat[order]  45.5 us
    gather x1, local copies, waits for them, and re-layouts, on_device(): cell_flat[order]  45.5 us
    unnamed x31, local copies, waits for them, and re-layouts  35.1 us
    mul x16, other arithmetic, kernel_weight(): return 0.25 * (1.0 + jnp.cos(0.5 * math.pi * distance))  20.8 us
  transfers between devices with their start and end apart: 10, of which 4 were waited for; matrix products, arithmetic and copies ran while one was open for 35% of the time, Pallas kernels for 0%

commit v1 on v0

v1 whole, which is shorter than its diff:
```python
import math

import jax
import jax.numpy as jnp
from jax import lax
from jax.experimental import pallas as pl
from jax.experimental.pallas import tpu as pltpu
from jax.sharding import PartitionSpec as P

relax_time = 0.8
velocity_x = [0, 1, -1, 0, 0, 0, 1, -1, 0, 0, 0, 1, -1, 0, 0, 1, 1, -1, -1]
velocity_y = [0, 0, 0, 1, -1, 0, 0, 0, 1, -1, 0, 0, 0, 1, -1, 1, -1, 1, -1]
velocity_z = [1, 1, 1, 1, 1, -1, -1, -1, -1, -1, 0, 0, 0, 0, 0, 0, 0, 0, 0]
lattice_weights = [
    1.0 / 18,
    1.0 / 36,
    1.0 / 36,
    1.0 / 36,
    1.0 / 36,
    1.0 / 18,
    1.0 / 36,
    1.0 / 36,
    1.0 / 36,
    1.0 / 36,
    1.0 / 3,
    1.0 / 18,
    1.0 / 18,
    1.0 / 18,
    1.0 / 18,
    1.0 / 36,
    1.0 / 36,
    1.0 / 36,
    1.0 / 36,
]


def passed_along(value, axis, steps):
    count = lax.axis_size(axis)
    pairs = [(source, (source + steps) % count) for source in range(count)]
    return lax.ppermute(value, axis, pairs)


def with_halo(x, axis, dim, width):
    devices, length = (lax.axis_size(axis), x.shape[dim])
    up = [(i, i + 1) for i in range(devices - 1)]
    down = [(j, i) for i, j in up]
    last = lax.slice_in_dim(x, length - width, length, axis=dim)
    initial = lax.slice_in_dim(x, 0, width, axis=dim)
    before = lax.ppermute(last, axis, up)
    after = lax.ppermute(initial, axis, down)
    return jnp.concatenate([before, x, after], axis=dim)


def laplacian(padded):
    center = padded[:, :, 1:-1]
    return (
        padded[:, :, 2:]
        + padded[:, :, :-2]
        + jnp.roll(center, 1, 3)
        + jnp.roll(center, -1, 3)
        - 4.0 * center
    )


def membrane(displacement, tension, bending):
    padded = with_halo(displacement, "shard", 2, 2)
    wide_first = laplacian(padded)
    rows = wide_first.shape[2]
    place = lax.broadcasted_iota(jnp.int32, (1, 1, rows, 1), 2)
    index = lax.axis_index("shard")
    outside = ((place == 0) & (index == 0)) | (
        (place == rows - 1) & (index == lax.axis_size("shard") - 1)
    )
    wide_first = jnp.where(outside, 0.0, wide_first)
    second = laplacian(wide_first)
    first = wide_first[:, :, 1:-1]
    return tension[None, :, None, None] * first - bending[None, :, None, None] * second


WINDOW = 16
ROWS = 24
BLOCK = 256


def weights(fraction):
    angle = (0.5 * math.pi) * fraction
    c, s = jnp.cos(angle), jnp.sin(angle)
    return [0.25 * (1.0 - s), 0.25 * (1.0 + c), 0.25 * (1.0 + s), 0.25 * (1.0 - c)]


def prepared(listed, slab, width):
    key = listed[6].astype(jnp.int32)
    windows = width // WINDOW
    bounds = jnp.arange(windows + 1, dtype=jnp.int32) * (WINDOW * slab * width)
    starts = jnp.sum((key[None, :] < bounds[:, None]).astype(jnp.int32), 1)
    x = key // (slab * width)
    plane = key // width % slab
    y = key % width
    values = jnp.stack(
        [listed[0], listed[1], listed[2]]
        + weights(listed[3])
        + weights(listed[4])
        + weights(listed[5])
        + [jnp.zeros_like(listed[0])],
        0,
    )
    places = jnp.stack([x, plane, y] + [jnp.zeros_like(x)] * 5, 0)
    return starts, values, places


def spread_list(starts, values_ref, places_ref, acc, shift, planes, width):
    windows = width // WINDOW
    row_id = lax.broadcasted_iota(jnp.int32, (ROWS, BLOCK), 0)
    y_id = lax.broadcasted_iota(jnp.int32, (width, BLOCK), 0)

    def pick(rel, parts):
        result = jnp.zeros(rel.shape, jnp.float32)
        for k in range(4):
            result = jnp.where(rel == k, parts[k], result)
        return result

    @pl.loop(0, windows)
    def _(w):
        begin = starts[w] // BLOCK
        end = (starts[w + 1] + (BLOCK - 1)) // BLOCK
        base = w * WINDOW

        @pl.loop(begin, end)
        def _(b):
            at = pl.ds(pl.multiple_of(b * BLOCK, BLOCK), BLOCK)

            def value(r):
                return values_ref[r : r + 1, at]

            x = places_ref[0:1, at] - base
            x = jnp.where((x >= 0) & (x < WINDOW), x, 4 * ROWS)
            plane = places_ref[1:2, at]
            y = places_ref[2:3, at]
            weight_x = pick(row_id - x, [value(3 + k) for k in range(4)])
            right = pick(
                (y_id - y + 1) & (width - 1), [value(7 + k) for k in range(4)]
            ).astype(jnp.bfloat16)
            lefts = []
            for q in planes:
                weight_z = pick(q + 1 + shift - plane, [value(11 + k) for k in range(4)])
                for c in range(3):
                    lefts.append((value(c) * weight_z) * weight_x)
            left = jnp.concatenate(lefts, 0).astype(jnp.bfloat16)
            product = lax.dot_general(
                left, right, (((1,), (1,)), ((), ())), preferred_element_type=jnp.float32
            )
            rows = pl.ds(pl.multiple_of(base, 8), ROWS)
            for n, q in enumerate(planes):
                for c in range(3):
                    i = n * 3 + c
                    acc[q * 3 + c, rows, :] += product[i * ROWS : (i + 1) * ROWS]


def spread_own(own, slab, width):
    starts, values, places = own

    def kernel(starts_ref, values_ref, places_ref, acc):
        acc[...] = jnp.zeros_like(acc)
        spread_list(starts_ref, values_ref, places_ref, acc, 0, range(slab), width)

    vmem = pl.BlockSpec(memory_space=pltpu.VMEM)
    return pl.pallas_call(
        kernel,
        out_shape=jax.ShapeDtypeStruct((slab * 3, width + ROWS - WINDOW, width), jnp.float32),
        in_specs=[pl.BlockSpec(memory_space=pltpu.SMEM), vmem, vmem],
        out_specs=vmem,
        name="spread_own",
        cost_estimate=pl.CostEstimate(
            flops=20_000_000_000, bytes_accessed=4_000_000, transcendentals=0
        ),
    )(starts, values, places)


def spread_others(total, below, above, slab, width):
    def kernel(s0, v0, p0, s1, v1, p1, total_ref, out, acc):
        acc[...] = total_ref[...]
        spread_list(s0, v0, p0, acc, slab, (0, 1), width)
        spread_list(s1, v1, p1, acc, -slab, (slab - 1,), width)
        for i in range(slab * 3):
            out[i] = acc[i, 1 : width + 1, :]
            out[i, width - 1 : width, :] += acc[i, 0:1, :]
            out[i, 0:2, :] += acc[i, width + 1 : width + 3, :]

    vmem = pl.BlockSpec(memory_space=pltpu.VMEM)
    smem = pl.BlockSpec(memory_space=pltpu.SMEM)
    return pl.pallas_call(
        kernel,
        out_shape=jax.ShapeDtypeStruct((slab * 3, width, width), jnp.float32),
        in_specs=[smem, vmem, vmem, smem, vmem, vmem, vmem],
        out_specs=vmem,
        scratch_shapes=[pltpu.VMEM(total.shape, jnp.float32)],
        name="spread_others",
        cost_estimate=pl.CostEstimate(
            flops=20_000_000_000, bytes_accessed=6_000_000, transcendentals=0
        ),
    )(*below, *above, total)


def dispatched(membrane_force, offset, owner, cell, device_count, cells):
    point_count = owner.size
    capacity = 2 * point_count // device_count
    slot_total = device_count * capacity
    owner = owner.reshape(point_count)
    cell = cell.reshape(point_count)
    devices = jnp.arange(device_count, dtype=jnp.int32)
    counts = jnp.sum((owner[None, :] == devices[:, None]).astype(jnp.int32), 1)
    filler_ends = jnp.cumsum(capacity - counts)
    filler = jnp.arange(slot_total - point_count, dtype=jnp.int32)
    filler_owner = jnp.sum((filler[None, :] >= filler_ends[:, None]).astype(jnp.int32), 0)
    span = 2 * cells
    key = jnp.concatenate([owner * span + cell, filler_owner * span + cells])
    payload = jnp.concatenate(
        [membrane_force.reshape(3, point_count), offset.reshape(3, point_count)], 0
    )
    payload = jnp.pad(payload, ((0, 0), (0, slot_total - point_count)))
    ordered = lax.sort(
        (key,) + tuple(payload[i] for i in range(6)), num_keys=1, is_stable=False
    )
    tag = (ordered[0] % span).astype(jnp.float32)
    send = jnp.stack(
        [v.reshape(device_count, capacity) for v in list(ordered[1:]) + [tag]], 1
    )
    got = lax.all_to_all(send, ("ves", "shard"), split_axis=0, concat_axis=0, tiled=True)
    return got.transpose(1, 0, 2).reshape(7, slot_total)


def collide(populations, field):
    density = jnp.sum(populations, 1)
    moment_x = jnp.zeros_like(density)
    moment_y = jnp.zeros_like(density)
    moment_z = jnp.zeros_like(density)
    for item in range(19):
        moment_x = moment_x + velocity_x[item] * populations[:, item]
        moment_y = moment_y + velocity_y[item] * populations[:, item]
        moment_z = moment_z + velocity_z[item] * populations[:, item]
    flow_x = (moment_x + 0.5 * field[:, 0]) / density
    flow_y = (moment_y + 0.5 * field[:, 1]) / density
    flow_z = (moment_z + 0.5 * field[:, 2]) / density
    speed_sq = flow_x * flow_x + flow_y * flow_y + flow_z * flow_z
    result = []
    for item in range(19):
        ex, ey, ez = (velocity_x[item], velocity_y[item], velocity_z[item])
        weight = lattice_weights[item]
        along = ex * flow_x + ey * flow_y + ez * flow_z
        equilibrium = weight * density * (1.0 + 3.0 * along + 4.5 * along * along - 1.5 * speed_sq)
        push = (
            (ex - flow_x) * field[:, 0] + (ey - flow_y) * field[:, 1] + (ez - flow_z) * field[:, 2]
        )
        facing = ex * field[:, 0] + ey * field[:, 1] + ez * field[:, 2]
        source = weight * (3.0 * push + 9.0 * along * facing)
        current = populations[:, item]
        result.append(
            current - (current - equilibrium) / relax_time + (1.0 - 0.5 / relax_time) * source
        )
    return jnp.stack(result, 1)


def on_device(displacement, tension, bending, offset, owner, cell, populations):
    membrane_force = membrane(displacement, tension, bending)
    device_count = lax.axis_size("ves") * lax.axis_size("shard")
    slab, width = (populations.shape[0], populations.shape[2])
    cells = slab * width * width
    got = dispatched(membrane_force, offset, owner, cell, device_count, cells)
    tag = got[6].astype(jnp.int32)
    plane, x, y = (tag // (width * width), tag // width % width, tag % width)
    key = jnp.where(tag >= cells, cells, (x * slab + plane) * width + y)
    ordered = lax.sort(
        (key,) + tuple(got[i] for i in range(6)), num_keys=1, is_stable=False
    )
    listed = jnp.stack(list(ordered[1:]) + [ordered[0].astype(jnp.float32)], 0)
    below = passed_along(listed, ("ves", "shard"), 1)
    above = passed_along(listed, ("ves", "shard"), -1)
    total = spread_own(prepared(listed, slab, width), slab, width)
    force_field = spread_others(
        total, prepared(below, slab, width), prepared(above, slab, width), slab, width
    ).reshape(slab, 3, width, width)
    post = collide(populations, force_field)
    low_part = passed_along(post[slab - 1, 0:5], ("ves", "shard"), 1)
    high_part = passed_along(post[0, 5:10], ("ves", "shard"), -1)
    low_source = jnp.concatenate([low_part[None], post[: slab - 1, 0:5]], 0)
    high_source = jnp.concatenate([post[1:, 5:10], high_part[None]], 0)
    source = jnp.concatenate([low_source, high_source, post[:, 10:]], 1)
    moved = [
        jnp.roll(source[:, item], (velocity_x[item], velocity_y[item]), (1, 2))
        for item in range(19)
    ]
    return (membrane_force, force_field, jnp.stack(moved, 1))


def solution(mesh):
    return jax.shard_map(
        on_device,
        mesh=mesh,
        in_specs=(
            P(None, "ves", "shard", None),
            P("ves"),
            P("ves"),
            P(None, "ves", "shard", None),
            P("ves", "shard", None),
            P("ves", "shard", None),
            P(("ves", "shard"), None, None, None),
        ),
        out_specs=(
            P(None, "ves", "shard", None),
            P(("ves", "shard"), None, None, None),
            P(("ves", "shard"), None, None, None),
        ),
        check_vma=False,
    )
```

time: 660 us -> 264 us (0.40); the launches traced: 647 us -> 262 us
  local copies, waits for them, and re-layouts: 214 us -> 22.2 us
  matrix products: 137 us -> 0 us
  other arithmetic: 153 us -> 87.1 us
  Pallas kernels: 0 us -> 57.3 us
  waiting for transfers between devices: 112 us -> 74.8 us
  starting transfers between devices: 28.4 us -> 18.4 us
    dot_general x16 -> x0, matrix products: 137 us -> none  [spread_block(): lax.dot_general(left, right, (((0,), (0,)), ((), ())), preferred_element_...]
    gather x2 -> x0, local copies, waits for them, and re-layouts: 91.1 us -> none  [the longest x1 45.5 us: on_device(): sorted_owner = owner_flat[order]]
    convert_element_type x16 -> x1, other arithmetic: 86.4 us -> 0.03 us  [dispatched(): tag = (ordered[0] % span).astype(jnp.float32)]
    scatter x1 -> x0, local copies, waits for them, and re-layouts: 70.4 us -> none  [on_device(): jnp.zeros((6, slot_total), jnp.float32).at[:, slot].set(payload[:, order])]
    pallas_call x0 -> x2, Pallas kernels: none -> 57.3 us  [the longest x1 40.7 us: spread_others(): pl.pallas_call(kernel, out_shape=jax.ShapeDtypeStruct((slab * 3, width, w...]
    unnamed x31 -> x20, local copies, waits for them, and re-layouts: 35.1 us -> 4.45 us
    ppermute x4, waiting for transfers between devices: 95.2 us -> 65.9 us  [passed_along(): return lax.ppermute(value, axis, pairs)]
    sort x1 -> x2, other arithmetic: 7.52 us -> 36.2 us  [the longest x1 22.8 us: on_device(): lax.sort((key,) + tuple((got[i] for i in range(6))), num_keys=1, is_stabl...]
  transfers between devices with their start and end apart: 10 -> 7, of which waited for: 4 -> 3; matrix products, arithmetic and copies ran while one was open for 35% -> 8% of each run, Pallas kernels for 0% -> 0%
where the time goes in v1:
time: 264 us; the launch traced here: 262 us
  other arithmetic  87.1 us (33%)
  waiting for transfers between devices  74.8 us (28%)
  Pallas kernels  57.3 us (22%)
  local copies, waits for them, and re-layouts  22.2 us (8%)
  starting transfers between devices  18.4 us (7%)
    ppermute x4, waiting for transfers between devices, passed_along(): return lax.ppermute(value, axis, pairs)  65.9 us
    pallas_call x1, Pallas kernels, spread_others(): pl.pallas_call(kernel, out_shape=jax.ShapeDtypeStruct((slab * 3, width, w...  40.7 us
    sort x1, other arithmetic, on_device(): lax.sort((key,) + tuple((got[i] for i in range(6))), num_keys=1, is_stabl...  22.8 us
    pallas_call x1, Pallas kernels, spread_own(): pl.pallas_call(kernel, out_shape=jax.ShapeDtypeStruct((slab * 3, width +...  16.7 us
    mul x5, other arithmetic, weights(): 0.25 * (1.0 - c)  14.2 us
    sort x1, other arithmetic, dispatched(): lax.sort((key,) + tuple((payload[i] for i in range(6))), num_keys=1, is_s...  13.4 us
    unnamed x23, other arithmetic  11.9 us
    add x4, other arithmetic, collide(): current - (current - equilibrium) / relax_time  9.77 us
  transfers between devices with their start and end apart: 7, of which 3 were waited for; matrix products, arithmetic and copies ran while one was open for 8% of the time, Pallas kernels for 0%

profile of v1, /device:TPU:14, one launch (start us, length us, event | category | flops | bytes accessed | tf_op | source)
XLA Modules:
  0.0 261.7 jit_solution(12759672242662655794)
XLA Ops:
  1.5 2.4 collective-permute-start
  3.9 4.3 %collective-permute-start.1 = (f32[3,2,2,128]{3,2,1,0:T(2,128)S(1)}, f32[3,2,2,128]{3,2,1,0:T(2,128)S(1)}, u32[]{:S(2)}, u32[]{:S(2)}) collective-permute-start(f32[3,2,2,128]{3,2,1,0:T(2,128)S(1)} %get-tuple-element.124), channel_id=1, source_target_pairs={{0,1},{1,2},{2,3},{3,4},{4,5},{5,6},{6,7},{8,9},{9,10},{10,11},{11... | collective-permute-start | bytes 18440 | tf_op jit(solution)/shard_map/ppermute | solution.py:49
  13.7 13.4 %sort.90 = (s32[16384]{0:T(1024)S(1)}, f32[16384]{0:T(1024)S(1)}, f32[16384]{0:T(1024)S(1)}, f32[16384]{0:T(1024)S(1)}, f32[16384]{0:T(1024)S(1)}, /*index=5*/f32[16384]{0:T(1024)S(1)}, f32[16384]{0:T(1024)S(1)}) sort(s32[16384]{0:T(1024)S(1)} %pad_add_fusion, f32[16384]{0:T(1024)S(1)} %bitcast.1388, f32[16384]{0:T(1024)S(1)} %bitcast.1387, ...), dimensions={0}, to_apply=%region_3.4 | sort | flops 229376 | bytes 917504 | tf_op jit(solution)/shard_map/sort | solution.py:221
  28.5 5.7 %all-to-all-start = ((f32[32,7,512]{2,1,0:T(8,128)}), f32[32,7,512]{2,1,0:T(8,128)S(1)}, u32[]{:S(2)}, u32[]{:S(2)}) async-start(f32[32,7,512]{2,1,0:T(8,128)} %stack.98), calls=%async_computation | async-start | bytes 1048576 | tf_op jit(solution)/shard_map/all_to_all | solution.py:228
  34.1 4.5 %reduce_sum.61 = f32[2,256,256]{2,1,0:T(8,128)S(1)} reduce(f32[2,19,256,256]{3,2,1,0:T(8,128)} %param.13, f32[]{:T(128)} %constant.206.clone.1), dimensions={1}, to_apply=%region_8.9 | reduce | flops 2359296 | bytes 10485764 | tf_op jit(solution)/shard_map/reduce_sum | solution.py:233
  38.7 8.9 %all-to-all-done = f32[32,7,512]{2,1,0:T(8,128)S(1)} async-done(((f32[32,7,512]{2,1,0:T(8,128)}), f32[32,7,512]{2,1,0:T(8,128)S(1)}, u32[]{:S(2)}, u32[]{:S(2)}) %all-to-all-start) | async-done | bytes 458784 | tf_op jit(solution)/shard_map/all_to_all | solution.py:228
  48.0 22.8 %sort.91 = (s32[16384]{0:T(1024)S(1)}, f32[16384]{0:T(1024)S(1)}, f32[16384]{0:T(1024)S(1)}, f32[16384]{0:T(1024)S(1)}, f32[16384]{0:T(1024)S(1)}, /*index=5*/f32[16384]{0:T(1024)S(1)}, f32[16384]{0:T(1024)S(1)}) sort(s32[16384]{0:T(1024)S(1)} %fusion.347, f32[16384]{0:T(1024)S(1)} %bitcast.1367, f32[16384]{0:T(1024)S(1)} %bitcast.1366, ...), dimensions={0}, to_apply=%region_4.5 | sort | flops 229376 | bytes 917504 | tf_op jit(solution)/shard_map/sort | solution.py:272
  72.2 1.6 collective-permute-start.3
  73.8 1.4 collective-permute-start.2
  78.1 3.0 %stack.224.values_ref = f32[16,16384]{1,0:T(8,128)} concatenate(f32[1,16384]{1,0:T(1,128)S(1)} %bitcast.1393, f32[1,16384]{1,0:T(1,128)S(1)} %bitcast.1395, f32[1,16384]{1,0:T(1,128)S(1)} %bitcast.1397, f32[1,16384]{1,0:T(1,128)S(1)} %bitcast.1373, f32[1,16384]{1,0:T(1,128)S(1)} %bitcast.1372, f32[1,16384]{1,0:T(1,128)S(1)} %bitcast.1371, f32[1,16384]{1,0:T(1,128)S(1)} %bitcast.1370, ...), dimensions={0} | concatenate | bytes 2097152 | tf_op jit(solution)/shard_map/stack | solution.py:99
  81.1 16.5 %collective-permute-done.2 = f32[7,16384]{1,0:T(8,128)S(1)} collective-permute-done((f32[7,16384]{1,0:T(8,128)S(1)}, f32[7,16384]{1,0:T(8,128)S(1)}, u32[]{:S(2)}, u32[]{:S(2)}) %collective-permute-start.2) | collective-permute-done | bytes 458784 | tf_op jit(solution)/shard_map/ppermute | solution.py:40
  102.1 6.3 %subtract_multiply_fusion.6 = (f32[1,16384]{1,0:T(1,128)S(1)}, f32[1,16384]{1,0:T(1,128)S(1)}, f32[1,16384]{1,0:T(1,128)S(1)}, f32[1,16384]{1,0:T(1,128)S(1)}, f...) fusion(f32[7,16384]{1,0:T(8,128)S(1)} %collective-permute-done.3), kind=kLoop, calls=%fused_computation.637 | loop fusion | flops 458752 | bytes 1114112 | tf_op jit(solution)/shard_map/mul | solution.py:88
  108.3 6.3 %subtract_multiply_fusion.12 = (f32[1,16384]{1,0:T(1,128)S(1)}, f32[1,16384]{1,0:T(1,128)S(1)}, f32[1,16384]{1,0:T(1,128)S(1)}, f32[1,16384]{1,0:T(1,128)S(1)}, ...) fusion(f32[7,16384]{1,0:T(8,128)S(1)} %collective-permute-done.2), kind=kLoop, calls=%fused_computation.649 | loop fusion | flops 458752 | bytes 1114112 | tf_op jit(solution)/shard_map/mul | solution.py:88
  115.9 16.7 %spread_own.1.total_ref = f32[6,264,256]{2,1,0:T(8,128)} custom-call(s32[17]{0:T(128)} %get-tuple-element.31.starts_ref, f32[16,16384]{1,0:T(8,128)} %stack.224.values_ref, s32[8,16384]{1,0:T(8,128)} %stack.228.places_ref), custom_call_target="tpu_custom_call" | custom-call | flops 20000000000 | bytes 4000000 | tf_op jit(solution)/shard_map/spread_own/pallas_call | solution.py:167
  132.6 2.8 %stack.208.v0 = f32[16,16384]{1,0:T(8,128)} concatenate(f32[3,16384]{1,0:T(4,128)S(1)} %slice.723, f32[1,16384]{1,0:T(1,128)S(1)} %get-tuple-element.101, f32[1,16384]{1,0:T(1,128)S(1)} %get-tuple-element.98, f32[1,16384]{1,0:T(1,128)S(1)} %get-tuple-element.92, f32[1,16384]{1,0:T(1,128)S(1)} %get-tuple-element.91, f32[1,16384]{1,0:T(1,128)S(1)} %get-tuple-element.100, ...), dimensions={0} | concatenate | bytes 2097152 | tf_op jit(solution)/shard_map/stack | solution.py:99
  135.4 2.8 %stack.210.v1 = f32[16,16384]{1,0:T(8,128)} concatenate(f32[3,16384]{1,0:T(4,128)S(1)} %slice.728, f32[1,16384]{1,0:T(1,128)S(1)} %get-tuple-element.86, f32[1,16384]{1,0:T(1,128)S(1)} %get-tuple-element.83, f32[1,16384]{1,0:T(1,128)S(1)} %get-tuple-element.77, f32[1,16384]{1,0:T(1,128)S(1)} %get-tuple-element.76, f32[1,16384]{1,0:T(1,128)S(1)} %get-tuple-element.85, ...), dimensions={0} | concatenate | bytes 2097152 | tf_op jit(solution)/shard_map/stack | solution.py:99
  138.2 40.7 %spread_others.1 = f32[6,256,256]{2,1,0:T(8,128)} custom-call(s32[17]{0:T(128)} %get-tuple-element.33.s0, f32[16,16384]{1,0:T(8,128)} %stack.208.v0, s32[8,16384]{1,0:T(8,128)} %stack.209.p0, s32[17]{0:T(128)} %get-tuple-element.32.s1, f32[16,16384]{1,0:T(8,128)} %stack.210.v1, s32[8,16384]{1,0:T(8,128)} %stack.211.p1, f32[6,264,256]{2,1,0:T(8,128)} %spread_own.1.total_ref), custom_call_target="tpu_custom_call" | custom-call | flops 20000000000 | bytes 6000000 | tf_op jit(solution)/shard_map/spread_others/pallas_call | solution.py:191
  178.9 5.6 %fusion.47 = (f32[2,5,256,256]{3,2,0,1:T(8,128)S(1)}, f32[2,1,256,256]{3,2,0,1:T(8,128)S(1)}, f32[2,1,256,256]{3,2,0,1:T(8,128)S(1)}, f32[2,1,256,256]{3,2,0,1:T(8,128)S(1)}) fusion(f32[2,256,256]{2,1,0:T(8,128)S(1)} %reduce_sum.61, f32[2,19,256,256]{3,2,1,0:T(8,128)} %param.13, f32[2,3,256,256]{3,2,1,0:T(8,128)} %bitcast.1333), kind=kLoop, calls=%fused_computation.92 | loop fusion | flops 17694720 | bytes 14155776
  184.5 5.9 %fusion.144 = (f32[2,256,256]{2,1,0:T(8,128)S(1)}, f32[2,256,256]{2,1,0:T(8,128)S(1)}, f32[2,256,256]{2,1,0:T(8,128)S(1)}, f32[2,256,256]{2,1,0:T(8,128)S(1)}) fusion(f32[2,256,256]{2,1,0:T(8,128)S(1)} %reduce_sum.61, f32[2,19,256,256]{3,2,1,0:T(8,128)} %param.13, f32[2,3,256,256]{3,2,1,0:T(8,128)S(1)} %bitcast.1335), kind=kLoop, calls=%fused_computation.189 | loop fusion | flops 17694720 | bytes 14155776 | tf_op jit(solution)/shard_map/add | solution.py:258
  195.7 3.0 %collective-permute-start.4 = (f32[5,256,256]{2,1,0:T(8,128)S(1)}, f32[5,256,256]{2,1,0:T(8,128)S(1)}, u32[]{:S(2)}, u32[]{:S(2)}) collective-permute-start(f32[5,256,256]{2,1,0:T(8,128)S(1)} %get-tuple-element.72), channel_id=1, source_target_pairs={{0,1},{1,2},{2,3},{3,4},{4,5},{5,6},{6,7},{7,8},{8,9},{9,10},{10,1... | collective-permute-start | bytes 3932168 | tf_op jit(solution)/shard_map/ppermute | solution.py:40
  198.7 1.7 fusion.130
  200.4 1.6 fusion.137
  203.9 49.5 %collective-permute-done.4 = f32[5,256,256]{2,1,0:T(8,128)S(1)} collective-permute-done((f32[5,256,256]{2,1,0:T(8,128)S(1)}, f32[5,256,256]{2,1,0:T(8,128)S(1)}, u32[]{:S(2)}, u32[]{:S(2)}) %collective-permute-start.4) | collective-permute-done | bytes 1310752 | tf_op jit(solution)/shard_map/ppermute | solution.py:40
  257.4 3.9 %copy-done.4 = f32[2,19,256,256]{3,2,1,0:T(8,128)} copy-done((f32[2,19,256,256]{3,2,1,0:T(8,128)}, f32[2,19,256,256]{3,2,1,0:T(8,128)S(1)}, u32[]{:S(2)}) %copy-start.4) | copy-done | bytes 9961496
  (124 shorter events, 29.1 us)
Async XLA Ops:
  0.6 12.3 %copy-start.5 = (f32[2]{0:T(128)S(1)}, f32[2]{0:T(128)}, u32[]{:S(2)}) copy-start(f32[2]{0:T(128)} %param.9) | copy-start | bytes 28
  0.6 12.3 %copy-start.6 = (f32[2]{0:T(128)S(1)}, f32[2]{0:T(128)}, u32[]{:S(2)}) copy-start(f32[2]{0:T(128)} %param.8) | copy-start | bytes 28
  0.7 12.5 %copy-start.3 = (f32[3,2,32,128]{3,2,1,0:T(8,128)S(1)}, f32[3,2,32,128]{3,2,1,0:T(8,128)}, u32[]{:S(2)}) copy-start(f32[3,2,32,128]{3,2,1,0:T(8,128)} %param.10) | copy-start | bytes 294916
  1.5 9.1 %collective-permute-start = (f32[3,2,2,128]{3,2,1,0:T(2,128)S(1)}, f32[3,2,2,128]{3,2,1,0:T(2,128)S(1)}, u32[]{:S(2)}, u32[]{:S(2)}) collective-permute-start(f32[3,2,2,128]{3,2,1,0:T(2,128)S(1)} %get-tuple-element.125), channel_id=1, source_target_pairs={{1,0},{2,1},{3,2},{4,3},{5,4},{6,5},{7,6},{9,8},{10,9},{11,10},{12... | collective-permute-start | bytes 18440 | tf_op jit(solution)/shard_map/ppermute | solution.py:50
  3.9 6.7 %collective-permute-start.1 = (f32[3,2,2,128]{3,2,1,0:T(2,128)S(1)}, f32[3,2,2,128]{3,2,1,0:T(2,128)S(1)}, u32[]{:S(2)}, u32[]{:S(2)}) collective-permute-start(f32[3,2,2,128]{3,2,1,0:T(2,128)S(1)} %get-tuple-element.124), channel_id=1, source_target_pairs={{0,1},{1,2},{2,3},{3,4},{4,5},{5,6},{6,7},{8,9},{9,10},{10,11},{11... | collective-permute-start | bytes 18440 | tf_op jit(solution)/shard_map/ppermute | solution.py:49
  13.1 25.5 %copy-start.1 = (f32[3,2,32,128]{3,2,1,0:T(8,128)}, f32[3,2,32,128]{3,2,1,0:T(8,128)S(1)}, u32[]{:S(2)}) copy-start(f32[3,2,32,128]{3,2,1,0:T(8,128)S(1)} %fusion.339) | copy-start | bytes 294916
  28.5 19.1 %all-to-all-start = ((f32[32,7,512]{2,1,0:T(8,128)}), f32[32,7,512]{2,1,0:T(8,128)S(1)}, u32[]{:S(2)}, u32[]{:S(2)}) async-start(f32[32,7,512]{2,1,0:T(8,128)} %stack.98), calls=%async_computation | async-start | bytes 1048576 | tf_op jit(solution)/shard_map/all_to_all | solution.py:228
  70.8 0.6 copy-start.2
  72.2 27.6 %collective-permute-start.3 = (f32[7,16384]{1,0:T(8,128)S(1)}, f32[7,16384]{1,0:T(8,128)S(1)}, u32[]{:S(2)}, u32[]{:S(2)}) collective-permute-start(f32[7,16384]{1,0:T(8,128)S(1)} %stack.207), channel_id=1, source_target_pairs={{0,31},{1,0},{2,1},{3,2},{4,3},{5,4},{6,5},{7,6},{8,7},{9,8},{10,9... | collective-permute-start | bytes 1376264 | tf_op jit(solution)/shard_map/ppermute | solution.py:40
  73.8 23.8 %collective-permute-start.2 = (f32[7,16384]{1,0:T(8,128)S(1)}, f32[7,16384]{1,0:T(8,128)S(1)}, u32[]{:S(2)}, u32[]{:S(2)}) collective-permute-start(f32[7,16384]{1,0:T(8,128)S(1)} %stack.207), channel_id=1, source_target_pairs={{0,1},{1,2},{2,3},{3,4},{4,5},{5,6},{6,7},{7,8},{8,9},{9,10},{10,1... | collective-permute-start | bytes 1376264 | tf_op jit(solution)/shard_map/ppermute | solution.py:40
  178.9 5.6 %copy-start = (f32[6,256,256]{2,1,0:T(8,128)S(1)}, f32[6,256,256]{2,1,0:T(8,128)}, u32[]{:S(2)}) copy-start(f32[6,256,256]{2,1,0:T(8,128)} %spread_others.1) | copy-start | bytes 4718596
  178.9 11.5 %slice-start = ((s8[9961472]{0:T(1024)(128)(4,1)}), s8[4194304]{0:T(1024)(128)(4,1)S(1)}, s32[]{:S(2)}) async-start(s8[9961472]{0:T(1024)(128)(4,1)} %bitcast.1345), calls=%async_computation.1 | async-start | bytes 8388608
  178.9 11.5 %slice-start.1 = ((s8[9961472]{0:T(1024)(128)(4,1)}), s8[4194304]{0:T(1024)(128)(4,1)S(1)}, s32[]{:S(2)}) async-start(s8[9961472]{0:T(1024)(128)(4,1)} %bitcast.1345), calls=%async_computation.2 | async-start | bytes 8388608
  184.5 5.9 %slice-start.2 = ((s8[9961472]{0:T(1024)(128)(4,1)}), s8[1572864]{0:T(1024)(128)(4,1)S(1)}, s32[]{:S(2)}) async-start(s8[9961472]{0:T(1024)(128)(4,1)} %bitcast.1345), calls=%async_computation.3 | async-start | bytes 3145728
  195.5 59.0 %collective-permute-start.5 = (f32[5,256,256]{2,1,0:T(8,128)S(1)}, f32[5,256,256]{2,1,0:T(8,128)S(1)}, u32[]{:S(2)}, u32[]{:S(2)}) collective-permute-start(f32[5,256,256]{2,1,0:T(8,128)S(1)} %get-tuple-element.65), channel_id=1, source_target_pairs={{0,31},{1,0},{2,1},{3,2},{4,3},{5,4},{6,5},{7,6},{8,7},{9,8},{10,9... | collective-permute-start | bytes 3932168 | tf_op jit(solution)/shard_map/ppermute | solution.py:40
  195.7 57.6 %collective-permute-start.4 = (f32[5,256,256]{2,1,0:T(8,128)S(1)}, f32[5,256,256]{2,1,0:T(8,128)S(1)}, u32[]{:S(2)}, u32[]{:S(2)}) collective-permute-start(f32[5,256,256]{2,1,0:T(8,128)S(1)} %get-tuple-element.72), channel_id=1, source_target_pairs={{0,1},{1,2},{2,3},{3,4},{4,5},{5,6},{6,7},{7,8},{8,9},{9,10},{10,1... | collective-permute-start | bytes 3932168 | tf_op jit(solution)/shard_map/ppermute | solution.py:40
  257.4 3.9 %copy-start.4 = (f32[2,19,256,256]{3,2,1,0:T(8,128)}, f32[2,19,256,256]{3,2,1,0:T(8,128)S(1)}, u32[]{:S(2)}) copy-start(f32[2,19,256,256]{3,2,1,0:T(8,128)S(1)} %fusion.164) | copy-start | bytes 29884420
